TPU v7x, 32 devices: a whole 2x2x4 slice. The times are simulated.
32 devices in a mesh: groups: 2 (over y), span: 4 (over x, core), head: 4 (over z).
Axes of the slice: x: 2, y: 2, z: 4, core: 2. Of those that a mesh axis runs over, the one named last changes fastest.
Arguments:
- queries: bfloat16 [4096, 1024], P(('groups', 'span', 'head')), parts along dimension 0, may hold values from -8 to 8
- keys: bfloat16 [4096, 1024], P(('groups', 'span', 'head')), parts along dimension 0, may hold values from -8 to 8
- values: bfloat16 [4096, 1024], P(('groups', 'span', 'head')), parts along dimension 0, may hold values from -6 to 6
- tile_offsets: int32 [32, 7], P(('groups', 'span')), parts along dimension 0, may hold values from 0 to 6, as said below
- timesteps: int32 [8], P(('groups', 'span')), parts along dimension 0, may hold values from 0 to 999
- time_weight: bfloat16 [256, 1024], P(None, 'head'), may hold values from -0.375 to 0.375
Outputs:
- attended: bfloat16 [4096, 1024], P(('groups', 'span', 'head')), parts along dimension 0
There are 2 independent parts, one for each index of `groups`. A program takes and returns all parts, laid end to end along the dimension named above; an argument that names none is the same for every part. Nothing has to cross between parts.
Inputs may be any that keep to these rules, and one draw needn't show every extreme that they name: `tile_offsets`: the first entry of each row is 0 and the 7 entries of a row are distinct.
All inputs are finite; a program needn't handle non-finite values.
Results may differ from a plain program's by a relative error of at most 0.0035.
Values may be sent and summed in bfloat16 or wider, within the bound.
No kernel may reach another device: no remote copies, remote signals or barrier semaphores. Data moves between devices by JAX's collectives and lax.ppermute only.
A program may use at most 64 MiB of HBM per device.

v0:
```python
import math
import jax
import jax.numpy as jnp
from jax import lax
from jax.sharding import PartitionSpec as P

HEAD_SIZE = 128
TILE = 128
FREQ = 256


def shifted(value, axis, by):
    size = lax.axis_size(axis)
    pairs = [(i, i + by) for i in range(size) if 0 <= i + by < size]
    return lax.ppermute(value, axis, pairs)


def local(queries, keys, values, tile_offsets, timesteps, time_weight):
    query_heads, key_heads, value_heads = (
        lax.all_to_all(queries, "head", split_axis=1, concat_axis=0, tiled=True),
        lax.all_to_all(keys, "head", split_axis=1, concat_axis=0, tiled=True),
        lax.all_to_all(values, "head", split_axis=1, concat_axis=0, tiled=True),
    )
    span_rows = query_heads.shape[0]
    width = query_heads.shape[1]
    heads_here = width // HEAD_SIZE
    tiles_here = span_rows // TILE
    reach = 3 * tiles_here // 2
    listed = tile_offsets.shape[1]
    tail_rows = (reach - tiles_here) * TILE
    resident = jnp.concatenate([key_heads, value_heads], axis=1)
    nearer = shifted(resident, "span", 1)
    farther = shifted(resident[span_rows - tail_rows :], "span", 2)
    window = jnp.concatenate([farther, nearer, resident], axis=0)
    window = window.reshape(reach + tiles_here, TILE, 2 * width)
    half = FREQ // 2
    freqs = jnp.exp(-math.log(10000.0) * jnp.arange(half, dtype=jnp.float32) / half)
    angles = timesteps.astype(jnp.float32)[:, None] * freqs[None, :]
    embedded = jnp.concatenate([jnp.cos(angles), jnp.sin(angles)], axis=1)
    gate = jnp.dot(embedded, time_weight.astype(jnp.float32), precision=lax.Precision.HIGHEST)
    gate_rows = gate.reshape(1, 1, heads_here, HEAD_SIZE)
    position = lax.axis_index("span")
    scale = HEAD_SIZE ** (-0.5)
    query_blocks = query_heads.reshape(tiles_here // 4, 4, TILE, heads_here, HEAD_SIZE)
    offset_blocks = tile_offsets.reshape(tiles_here // 4, 4, listed)

    def one_block(inputs):
        block, query_part, offsets = inputs
        local_tiles = block * 4 + jnp.arange(4, dtype=jnp.int32)
        source = local_tiles[:, None] - offsets
        usable = position * tiles_here + source >= 0
        picked = window[source + reach].reshape(4, listed * TILE, 2 * width)
        key_part = picked[:, :, :width].reshape(4, listed * TILE, heads_here, HEAD_SIZE)
        value_part = picked[:, :, width:].reshape(4, listed * TILE, heads_here, HEAD_SIZE)
        scores = (
            jnp.einsum("qthd,qkhd->qhtk", query_part, key_part, preferred_element_type=jnp.float32)
            * scale
        )
        keep = jnp.repeat(usable, TILE, axis=1)
        scores = jnp.where(keep[:, None, None, :], scores, -1e30)
        top = jnp.max(scores, axis=-1, keepdims=True)
        weights = jnp.exp(scores - top)
        total = jnp.sum(weights, axis=-1, keepdims=True)
        rounded = weights.astype(jnp.bfloat16)
        mixed = jnp.einsum(
            "qhtk,qkhd->qthd", rounded, value_part, preferred_element_type=jnp.float32
        )
        mixed = mixed / jnp.transpose(total, (0, 2, 1, 3))
        return (mixed * (1.0 + gate_rows)).astype(jnp.bfloat16)

    blocks = jnp.arange(tiles_here // 4, dtype=jnp.int32)
    gated = lax.map(one_block, (blocks, query_blocks, offset_blocks)).reshape(span_rows, width)
    return lax.all_to_all(gated, "head", split_axis=0, concat_axis=1, tiled=True)


def solution(mesh):
    return jax.shard_map(
        local,
        mesh=mesh,
        in_specs=(
            P(("groups", "span", "head"), None),
            P(("groups", "span", "head"), None),
            P(("groups", "span", "head"), None),
            P(("groups", "span"), None),
            P(("groups", "span")),
            P(None, "head"),
        ),
        out_specs=P(("groups", "span", "head"), None),
        check_vma=False,
    )
```

profile of v0, /device:TPU:7, one launch (start us, length us, event | category | flops | bytes accessed | tf_op | source)
XLA Modules:
  0.0 76.2 jit_solution(9081810094877849396)
XLA Ops:
  0.0 1.8 %copy.18 = bf16[128,1024]{0,1:T(8,128)(2,1)} copy(bf16[128,1024]{1,0:T(8,128)(2,1)} %param.8) | data formatting | bytes 524288 | tf_op args[2]
  1.8 4.6 %all-to-all-start.1 = ((bf16[128,4,256]{0,2,1:T(8,128)(2,1)}), bf16[128,4,256]{0,2,1:T(8,128)(2,1)S(1)}, u32[]{:S(2)}, u32[]{:S(2)}) async-start(bf16[128,4,256]{0,2,1:T(8,128)(2,1)} %bitcast.3), calls=%async_computation.1 | async-start | bytes 524288 | tf_op jit(solution)/shard_map/all_to_all | solution.py:22
  6.4 1.8 %copy.16 = bf16[128,1024]{0,1:T(8,128)(2,1)} copy(bf16[128,1024]{1,0:T(8,128)(2,1)} %param.7) | data formatting | bytes 524288 | tf_op args[1]
  8.2 0.7 add_compare_fusion
  8.9 5.1 %all-to-all-done.1 = bf16[128,4,256]{0,2,1:T(8,128)(2,1)S(1)} async-done(((bf16[128,4,256]{0,2,1:T(8,128)(2,1)}), bf16[128,4,256]{0,2,1:T(8,128)(2,1)S(1)}, u32[]{:S(2)}, u32[]{:S(2)}) %all-to-all-start.1) | async-done | bytes 262176 | tf_op jit(solution)/shard_map/all_to_all | solution.py:22
  14.0 3.4 %all-to-all-start = ((bf16[128,4,256]{0,2,1:T(8,128)(2,1)}), bf16[128,4,256]{0,2,1:T(8,128)(2,1)S(1)}, u32[]{:S(2)}, u32[]{:S(2)}) async-start(bf16[128,4,256]{0,2,1:T(8,128)(2,1)} %bitcast), calls=%async_computation | async-start | bytes 524288 | tf_op jit(solution)/shard_map/all_to_all | solution.py:21
  17.4 0.1 broadcast_bitcast_fusion
  17.5 1.8 %copy.22 = bf16[128,1024]{0,1:T(8,128)(2,1)} copy(bf16[128,1024]{1,0:T(8,128)(2,1)} %param.6) | data formatting | bytes 524288 | tf_op args[0]
  19.9 0.1 fusion.27
  20.0 0.1 fusion.22
  20.1 0.2 copy.19
  20.3 2.7 %all-to-all-done = bf16[128,4,256]{0,2,1:T(8,128)(2,1)S(1)} async-done(((bf16[128,4,256]{0,2,1:T(8,128)(2,1)}), bf16[128,4,256]{0,2,1:T(8,128)(2,1)S(1)}, u32[]{:S(2)}, u32[]{:S(2)}) %all-to-all-start) | async-done | bytes 262176 | tf_op jit(solution)/shard_map/all_to_all | solution.py:21
  23.0 3.4 %all-to-all-start.2 = ((bf16[128,4,256]{0,2,1:T(8,128)(2,1)}), bf16[128,4,256]{0,2,1:T(8,128)(2,1)S(1)}, u32[]{:S(2)}, u32[]{:S(2)}) async-start(bf16[128,4,256]{0,2,1:T(8,128)(2,1)} %bitcast.10), calls=%async_computation.2 | async-start | bytes 524288 | tf_op jit(solution)/shard_map/all_to_all | solution.py:20
  26.4 0.1 copy.17
  26.6 1.3 %collective-permute-start.1 = (bf16[512,512]{1,0:T(8,128)(2,1)S(1)}, bf16[512,512]{1,0:T(8,128)(2,1)S(1)}, u32[]{:S(2)}, u32[]{:S(2)}) collective-permute-start(bf16[512,512]{1,0:T(8,128)(2,1)S(1)} %pad_maximum_fusion), channel_id=1, source_target_pairs={{0,4},{4,8},{8,12},{1,5},{5,9},{9,13},{2,6},{6,10},{10,14},{3,7},{... | collective-permute-start | bytes 1572872 | tf_op jit(solution)/shard_map/ppermute | solution.py:15
  27.9 0.0 copy-done.2
  27.9 0.1 reshape.97
  28.1 1.3 %collective-permute-start = (bf16[256,512]{1,0:T(8,128)(2,1)S(1)}, bf16[256,512]{1,0:T(8,128)(2,1)S(1)}, u32[]{:S(2)}, u32[]{:S(2)}) collective-permute-start(bf16[256,512]{1,0:T(8,128)(2,1)S(1)} %fusion.21), channel_id=1, source_target_pairs={{0,8},{4,12},{1,9},{5,13},{2,10},{6,14},{3,11},{7,15},{16,24},{20,... | collective-permute-start | bytes 786440 | tf_op jit(solution)/shard_map/ppermute | solution.py:15
  29.4 16.3 %collective-permute-done = bf16[256,512]{1,0:T(8,128)(2,1)S(1)} collective-permute-done((bf16[256,512]{1,0:T(8,128)(2,1)S(1)}, bf16[256,512]{1,0:T(8,128)(2,1)S(1)}, u32[]{:S(2)}, u32[]{:S(2)}) %collective-permute-start) | collective-permute-done | bytes 262176 | tf_op jit(solution)/shard_map/ppermute | solution.py:15
  45.7 0.0 collective-permute-done.1
  45.7 0.1 maximum_maximum_fusion
  45.8 2.6 %gather_fusion = bf16[28,128,512]{2,1,0:T(8,128)(2,1)} fusion(bf16[10,128,512]{2,1,0:T(8,128)(2,1)S(1)} %bitcast.73, s32[1024]{0:T(1024)S(1)} %pad_clamp_fusion), kind=kCustom, calls=%fused_computation | custom fusion | bytes 7340144 | tf_op jit(solution)/shard_map/while/body/eval_jaxpr/gather | solution.py:52
  48.5 3.6 %fusion.32 = (bf16[4,896,256]{2,1,0:T(8,128)(2,1)S(1)}, bf16[4,896,256]{2,1,0:T(8,128)(2,1)}) fusion(bf16[4,896,512]{2,1,0:T(8,128)(2,1)} %bitcast.74), kind=kLoop, calls=%fused_computation.40 | loop fusion | bytes 7340032 | tf_op jit(solution)/shard_map/while/body/eval_jaxpr/slice | solution.py:53
  52.0 3.6 %copy.20 = bf16[4,896,256]{1,2,0:T(8,128)(2,1)} copy(bf16[4,896,256]{2,1,0:T(8,128)(2,1)} %get-tuple-element.18) | data formatting | bytes 3670016 | tf_op jit(solution)/shard_map/while/body/eval_jaxpr/slice | solution.py:54
  55.6 2.4 %copy.21 = bf16[4,896,256]{1,2,0:T(8,128)(2,1)} copy(bf16[4,896,256]{2,1,0:T(8,128)(2,1)S(1)} %get-tuple-element.17) | data formatting | bytes 3670016 | tf_op jit(solution)/shard_map/while/body/eval_jaxpr/slice | solution.py:53
  58.0 0.0 all-to-all-done.2
  58.0 2.6 %bitcast_reduce_fusion = (f32[4,2,128]{2,1,0:T(2,128)S(1)}, f32[4,2,896,128]{3,2,1,0:T(8,128)S(1)}) fusion(pred[4,896]{1,0:T(4,128)(4,1)S(1)} %bitcast.88, bf16[4,896,2,128]{1,3,2,0:T(8,128)(2,1)} %bitcast.75, bf16[4,128,2,128]{1,3,2,0:T(8,128)(2,1)S(1)} %bitcast.86), kind=kOutput, calls=%fused_computation.2 | convolution fusion | flops 237632512 | bytes 5774848 | tf_op jit(solution)/shard_map/while/body/eval_jaxpr/qthd,qkhd->qhtk/dot_general | solution.py:56
  60.6 1.1 %fusion.1 = f32[4,2,128]{2,1,0:T(2,128)S(1)} fusion(f32[4,2,896,128]{3,2,1,0:T(8,128)S(1)} %get-tuple-element.20, f32[4,2,128]{2,1,0:T(2,128)S(1)} %get-tuple-element.19, pred[4,896]{1,0:T(4,128)(4,1)S(1)} %bitcast.89), kind=kLoop, calls=%fused_computation.5 | loop fusion | flops 3668992 | bytes 3681792 | tf_op jit(solution)/shard_map/while/body/eval_jaxpr/reduce_sum | solution.py:63
  61.7 0.0 copy-done.1
  61.7 1.3 %fusion.18 = bf16[4,128,2,128]{1,3,2,0:T(8,128)(2,1)S(1)} fusion(bf16[4,896,2,128]{1,3,2,0:T(8,128)(2,1)S(1)} %bitcast.82, f32[4,2,896,128]{3,2,1,0:T(8,128)S(1)} %get-tuple-element.20, f32[4,2,128]{2,1,0:T(2,128)S(1)} %get-tuple-element.19, pred[4,896]{1,0:T(4,128)(4,1)S(1)} %bitcast.90, f32[2,128]{1,0:T(2,128)S(1)} %broadcast_add_fusion, ...), kind=kOutput, calls=%fused_computation.16 | convolution fusion | flops 238944256 | bytes 5779968 | tf_op jit(solution)/shard_map/while/body/eval_jaxpr/qhtk,qkhd->qthd/dot_general | solution.py:65
  63.0 12.3 %all_to_all.73 = bf16[4,128,256]{1,2,0:T(8,128)(2,1)S(1)} all-to-all(bf16[4,128,256]{1,2,0:T(8,128)(2,1)S(1)} %bitcast.87), channel_id=1, replica_groups=mesh['groups'=2,'span'=4,'head'=4] {'head'}, dimensions={0} | all-to-all | bytes 524288 | tf_op jit(solution)/shard_map/all_to_all | solution.py:73
  75.4 0.8 %copy.32 = bf16[128,1024]{1,0:T(8,128)(2,1)} copy(bf16[128,1024]{0,1:T(8,128)(2,1)S(1)} %bitcast.85) | data formatting | bytes 524288 | tf_op jit(solution)/shard_map/all_to_all | solution.py:73
  (10 shorter events, 0.1 us)
Async XLA Ops:
  0.0 20.0 %copy-start = (bf16[256,256]{1,0:T(8,128)(2,1)S(1)}, bf16[256,256]{1,0:T(8,128)(2,1)}, u32[]{:S(2)}) copy-start(bf16[256,256]{1,0:T(8,128)(2,1)} %param.11) | copy-start | bytes 393220
  0.0 27.9 %copy-start.2 = (s32[4,7]{1,0:T(4,128)S(1)}, s32[4,7]{1,0:T(4,128)}, u32[]{:S(2)}) copy-start(s32[4,7]{1,0:T(4,128)} %param.9) | copy-start | bytes 340
  1.8 12.2 %all-to-all-start.1 = ((bf16[128,4,256]{0,2,1:T(8,128)(2,1)}), bf16[128,4,256]{0,2,1:T(8,128)(2,1)S(1)}, u32[]{:S(2)}, u32[]{:S(2)}) async-start(bf16[128,4,256]{0,2,1:T(8,128)(2,1)} %bitcast.3), calls=%async_computation.1 | async-start | bytes 524288 | tf_op jit(solution)/shard_map/all_to_all | solution.py:22
  14.0 9.0 %all-to-all-start = ((bf16[128,4,256]{0,2,1:T(8,128)(2,1)}), bf16[128,4,256]{0,2,1:T(8,128)(2,1)S(1)}, u32[]{:S(2)}, u32[]{:S(2)}) async-start(bf16[128,4,256]{0,2,1:T(8,128)(2,1)} %bitcast), calls=%async_computation | async-start | bytes 524288 | tf_op jit(solution)/shard_map/all_to_all | solution.py:21
  23.0 35.0 %all-to-all-start.2 = ((bf16[128,4,256]{0,2,1:T(8,128)(2,1)}), bf16[128,4,256]{0,2,1:T(8,128)(2,1)S(1)}, u32[]{:S(2)}, u32[]{:S(2)}) async-start(bf16[128,4,256]{0,2,1:T(8,128)(2,1)} %bitcast.10), calls=%async_computation.2 | async-start | bytes 524288 | tf_op jit(solution)/shard_map/all_to_all | solution.py:20
  26.6 19.1 %collective-permute-start.1 = (bf16[512,512]{1,0:T(8,128)(2,1)S(1)}, bf16[512,512]{1,0:T(8,128)(2,1)S(1)}, u32[]{:S(2)}, u32[]{:S(2)}) collective-permute-start(bf16[512,512]{1,0:T(8,128)(2,1)S(1)} %pad_maximum_fusion), channel_id=1, source_target_pairs={{0,4},{4,8},{8,12},{1,5},{5,9},{9,13},{2,6},{6,10},{10,14},{3,7},{... | collective-permute-start | bytes 1572872 | tf_op jit(solution)/shard_map/ppermute | solution.py:15
  28.1 17.7 %collective-permute-start = (bf16[256,512]{1,0:T(8,128)(2,1)S(1)}, bf16[256,512]{1,0:T(8,128)(2,1)S(1)}, u32[]{:S(2)}, u32[]{:S(2)}) collective-permute-start(bf16[256,512]{1,0:T(8,128)(2,1)S(1)} %fusion.21), channel_id=1, source_target_pairs={{0,8},{4,12},{1,9},{5,13},{2,10},{6,14},{3,11},{7,15},{16,24},{20,... | collective-permute-start | bytes 786440 | tf_op jit(solution)/shard_map/ppermute | solution.py:15
  58.0 3.8 %copy-start.1 = (bf16[4,896,256]{1,2,0:T(8,128)(2,1)S(1)}, bf16[4,896,256]{1,2,0:T(8,128)(2,1)}, u32[]{:S(2)}) copy-start(bf16[4,896,256]{1,2,0:T(8,128)(2,1)} %copy.20) | copy-start | bytes 5505028
where the time goes:
time: 76.8 us; the launch traced here: 76.2 us
  waiting for transfers between devices  24.1 us (31%)
  local copies, waits for them, and re-layouts  18.9 us (25%)
  starting transfers between devices  14 us (18%)
  blocking collectives  12.3 us (16%)
  matrix products  4.02 us (5%)
  other arithmetic  2.02 us (3%)
  between operations  0.81 us (1%)
    ppermute x2, waiting for transfers between devices, shifted(): return lax.ppermute(value, axis, pairs)  16.3 us
    all_to_all x1, blocking collectives, local(): lax.all_to_all(gated, 'head', split_axis=0, concat_axis=1, tiled=True)  12.3 us
    slice x2, local copies, waits for them, and re-layouts, one_block(): picked[:, :, :width].reshape(4, listed * TILE, heads_here, HEAD_SIZE)  5.92 us
    unnamed x11, local copies, waits for them, and re-layouts  5.49 us
    all_to_all x1, waiting for transfers between devices, local(): lax.all_to_all(values, 'head', split_axis=1, concat_axis=0, tiled=True)  5.09 us
    all_to_all x1, starting transfers between devices, local(): lax.all_to_all(values, 'head', split_axis=1, concat_axis=0, tiled=True)  4.59 us
    slice x1, local copies, waits for them, and re-layouts, one_block(): picked[:, :, width:].reshape(4, listed * TILE, heads_here, HEAD_SIZE)  3.6 us
    all_to_all x1, starting transfers between devices, local(): lax.all_to_all(queries, 'head', split_axis=1, concat_axis=0, tiled=True)  3.41 us
  transfers between devices with their start and end apart: 5, of which 3 were waited for; matrix products, arithmetic and copies ran while one was open for 23% of the time, Pallas kernels for 0%

commit v1 on v0

--- a/solution.py
+++ b/solution.py
@@ -9,6 +9,18 @@
 FREQ = 256
 
 
+def sent_to_each(shard, axis, split, join):
+    ways, here = (lax.axis_size(axis), lax.axis_index(axis))
+    width = shard.shape[split] // ways
+    turned = jnp.roll(shard, -here * width, axis=split)
+    got = [lax.slice_in_dim(turned, 0, width, axis=split)]
+    for far in range(1, ways):
+        sent = lax.slice_in_dim(turned, far * width, (far + 1) * width, axis=split)
+        got.append(lax.ppermute(sent, axis, [(d, (d + far) % ways) for d in range(ways)]))
+    line = jnp.concatenate(got[::-1], axis=join)
+    return jnp.roll(line, (here + 1) * got[0].shape[join], axis=join)
+
+
 def shifted(value, axis, by):
     size = lax.axis_size(axis)
     pairs = [(i, i + by) for i in range(size) if 0 <= i + by < size]
@@ -18,7 +30,7 @@
 def local(queries, keys, values, tile_offsets, timesteps, time_weight):
     query_heads, key_heads, value_heads = (
         lax.all_to_all(queries, "head", split_axis=1, concat_axis=0, tiled=True),
-        lax.all_to_all(keys, "head", split_axis=1, concat_axis=0, tiled=True),
+        sent_to_each(keys, "head", 1, 0),
         lax.all_to_all(values, "head", split_axis=1, concat_axis=0, tiled=True),
     )
     span_rows = query_heads.shape[0]

time: 76.8 us -> 72.1 us (0.939)
  waiting for transfers between devices: 24.1 us -> 19.7 us
  local copies, waits for them, and re-layouts: 18.9 us -> 17.1 us
  other arithmetic: 2.02 us -> 3.08 us
    ppermute x0 -> x3, waiting for transfers between devices: none -> 5.34 us  [sent_to_each(): lax.ppermute(sent, axis, [(d, (d + far) % ways) for d in range(ways)])]
    all_to_all x1, waiting for transfers between devices: 5.09 us -> 0.01 us  [local(): lax.all_to_all(values, 'head', split_axis=1, concat_axis=0, tiled=True)]
    ppermute x0 -> x3, starting transfers between devices: none -> 3.9 us  [sent_to_each(): lax.ppermute(sent, axis, [(d, (d + far) % ways) for d in range(ways)])]
    all_to_all x1 -> x0, starting transfers between devices: 3.4 us -> none  [local(): lax.all_to_all(keys, 'head', split_axis=1, concat_axis=0, tiled=True)]
    all_to_all x1 -> x0, waiting for transfers between devices: 2.69 us -> none  [local(): lax.all_to_all(keys, 'head', split_axis=1, concat_axis=0, tiled=True)]
    unnamed x11 -> x17, local copies, waits for them, and re-layouts: 5.49 us -> 3.14 us
    ppermute x2, waiting for transfers between devices: 16.3 us -> 14.3 us  [shifted(): return lax.ppermute(value, axis, pairs)]
    concatenate x0 -> x1, other arithmetic: none -> 1.05 us  [sent_to_each(): turned = jnp.roll(shard, -here * width, axis=split)]
  transfers between devices with their start and end apart: 5 -> 7, of which waited for: 3 -> 2; matrix products, arithmetic and copies ran while one was open for 23% -> 23% of each run, Pallas kernels for 0% -> 0%
where the time goes in v1:
time: 72.1 us; the launch traced here: 71.6 us
  waiting for transfers between devices  19.7 us (27%)
  local copies, waits for them, and re-layouts  17.1 us (24%)
  starting transfers between devices  14.5 us (20%)
  blocking collectives  12.3 us (17%)
  matrix products  4.02 us (6%)
  other arithmetic  3.08 us (4%)
  between operations  0.88 us (1%)
    ppermute x2, waiting for transfers between devices, shifted(): return lax.ppermute(value, axis, pairs)  14.3 us
    all_to_all x1, blocking collectives, local(): lax.all_to_all(gated, 'head', split_axis=0, concat_axis=1, tiled=True)  12.3 us
    slice x2, local copies, waits for them, and re-layouts, one_block(): picked[:, :, :width].reshape(4, listed * TILE, heads_here, HEAD_SIZE)  5.89 us
    ppermute x3, waiting for transfers between devices, sent_to_each(): lax.ppermute(sent, axis, [(d, (d + far) % ways) for d in range(ways)])  5.34 us
    all_to_all x1, starting transfers between devices, local(): lax.all_to_all(values, 'head', split_axis=1, concat_axis=0, tiled=True)  4.59 us
    ppermute x3, starting transfers between devices, sent_to_each(): lax.ppermute(sent, axis, [(d, (d + far) % ways) for d in range(ways)])  3.9 us
    slice x1, local copies, waits for them, and re-layouts, one_block(): picked[:, :, width:].reshape(4, listed * TILE, heads_here, HEAD_SIZE)  3.56 us
    all_to_all x1, starting transfers between devices, local(): lax.all_to_all(queries, 'head', split_axis=1, concat_axis=0, tiled=True)  3.42 us
  transfers between devices with their start and end apart: 7, of which 2 were waited for; matrix products, arithmetic and copies ran while one was open for 23% of the time, Pallas kernels for 0%

profile of v1, /device:TPU:7, one launch (start us, length us, event | category | flops | bytes accessed | tf_op | source)
XLA Modules:
  0.0 71.6 jit_solution(5152904601564752032)
XLA Ops:
  0.0 1.2 %copy.25 = bf16[128,1024]{0,1:T(8,128)(2,1)S(1)} copy(bf16[128,1024]{1,0:T(8,128)(2,1)} %param.8) | data formatting | bytes 524288 | tf_op args[2]
  1.2 0.9 %copy.26 = bf16[128,4,256]{2,0,1:T(8,128)(2,1)} copy(bf16[128,4,256]{0,2,1:T(8,128)(2,1)S(1)} %bitcast.79) | data formatting | bytes 524288 | tf_op jit(solution)/shard_map/all_to_all | solution.py:34
  2.0 4.6 %all-to-all-start = ((bf16[128,4,256]{2,0,1:T(8,128)(2,1)}), bf16[128,4,256]{2,0,1:T(8,128)(2,1)S(1)}, u32[]{:S(2)}, u32[]{:S(2)}) async-start(bf16[128,4,256]{2,0,1:T(8,128)(2,1)} %copy.26), calls=%async_computation | async-start | bytes 524288 | tf_op jit(solution)/shard_map/all_to_all | solution.py:34
  6.6 1.1 %fusion.21 = bf16[128,1024]{1,0:T(8,128)(2,1)S(1)} fusion(s32[]{:T(128)S(6)} %select_n.40, bf16[128,1024]{1,0:T(8,128)(2,1)} %param.7), kind=kLoop, calls=%fused_computation.22 | loop fusion | flops 524288 | bytes 524292 | tf_op jit(solution)/shard_map/jit(_roll_dynamic)/concatenate | solution.py:15
  7.7 3.3 %collective-permute-start = (bf16[128,256]{1,0:T(8,128)(2,1)S(1)}, bf16[128,256]{1,0:T(8,128)(2,1)S(1)}, u32[]{:S(2)}, u32[]{:S(2)}) collective-permute-start(bf16[128,256]{1,0:T(8,128)(2,1)S(1)} %get-tuple-element.28), channel_id=1, source_target_pairs={{0,3},{1,0},{2,1},{3,2},{4,7},{5,4},{6,5},{7,6},{8,11},{9,8},{10,9... | collective-permute-start | bytes 196616 | tf_op jit(solution)/shard_map/ppermute | solution.py:19
  11.0 0.0 collective-permute-start.1
  11.0 0.6 collective-permute-start.2
  12.2 0.1 fusion.28
  12.3 0.7 add_compare_fusion
  13.0 0.1 fusion.23
  13.1 0.1 broadcast_bitcast_fusion
  13.2 1.9 %copy.29 = bf16[128,1024]{0,1:T(8,128)(2,1)} copy(bf16[128,1024]{1,0:T(8,128)(2,1)} %param.6) | data formatting | bytes 524288 | tf_op args[0]
  15.1 0.0 collective-permute-done
  15.1 5.3 %collective-permute-done.1 = bf16[128,256]{1,0:T(8,128)(2,1)S(1)} collective-permute-done((bf16[128,256]{1,0:T(8,128)(2,1)S(1)}, bf16[128,256]{1,0:T(8,128)(2,1)S(1)}, u32[]{:S(2)}, u32[]{:S(2)}) %collective-permute-start.1) | collective-permute-done | bytes 65568 | tf_op jit(solution)/shard_map/ppermute | solution.py:19
  20.4 0.0 collective-permute-done.2
  20.6 0.0 all-to-all-done
  20.6 3.4 %all-to-all-start.1 = ((bf16[128,4,256]{0,2,1:T(8,128)(2,1)}), bf16[128,4,256]{0,2,1:T(8,128)(2,1)S(1)}, u32[]{:S(2)}, u32[]{:S(2)}) async-start(bf16[128,4,256]{0,2,1:T(8,128)(2,1)} %bitcast.7), calls=%async_computation.1 | async-start | bytes 524288 | tf_op jit(solution)/shard_map/all_to_all | solution.py:32
  24.0 1.3 %collective-permute-start.4 = (bf16[512,512]{1,0:T(8,128)(2,1)S(1)}, bf16[512,512]{1,0:T(8,128)(2,1)S(1)}, u32[]{:S(2)}, u32[]{:S(2)}) collective-permute-start(bf16[512,512]{1,0:T(8,128)(2,1)S(1)} %pad_maximum_fusion), channel_id=1, source_target_pairs={{0,4},{4,8},{8,12},{1,5},{5,9},{9,13},{2,6},{6,10},{10,14},{3,7},{... | collective-permute-start | bytes 1572872 | tf_op jit(solution)/shard_map/ppermute | solution.py:27
  25.4 0.1 reshape.94
  25.5 1.3 %collective-permute-start.3 = (bf16[256,512]{1,0:T(8,128)(2,1)S(1)}, bf16[256,512]{1,0:T(8,128)(2,1)S(1)}, u32[]{:S(2)}, u32[]{:S(2)}) collective-permute-start(bf16[256,512]{1,0:T(8,128)(2,1)S(1)} %fusion.22), channel_id=1, source_target_pairs={{0,8},{4,12},{1,9},{5,13},{2,10},{6,14},{3,11},{7,15},{16,24},{20,... | collective-permute-start | bytes 786440 | tf_op jit(solution)/shard_map/ppermute | solution.py:27
  26.8 14.3 %collective-permute-done.3 = bf16[256,512]{1,0:T(8,128)(2,1)S(1)} collective-permute-done((bf16[256,512]{1,0:T(8,128)(2,1)S(1)}, bf16[256,512]{1,0:T(8,128)(2,1)S(1)}, u32[]{:S(2)}, u32[]{:S(2)}) %collective-permute-start.3) | collective-permute-done | bytes 262176 | tf_op jit(solution)/shard_map/ppermute | solution.py:27
  41.1 0.0 collective-permute-done.4
  41.2 0.1 maximum_maximum_fusion
  41.2 2.6 %gather_fusion = bf16[28,128,512]{2,1,0:T(8,128)(2,1)} fusion(bf16[10,128,512]{2,1,0:T(8,128)(2,1)S(1)} %bitcast.71, s32[1024]{0:T(1024)S(1)} %pad_clamp_fusion), kind=kCustom, calls=%fused_computation | custom fusion | bytes 7340144 | tf_op jit(solution)/shard_map/while/body/eval_jaxpr/gather | solution.py:64
  43.9 3.6 %fusion.33 = (bf16[4,896,256]{2,1,0:T(8,128)(2,1)S(1)}, bf16[4,896,256]{2,1,0:T(8,128)(2,1)}) fusion(bf16[4,896,512]{2,1,0:T(8,128)(2,1)} %bitcast.72), kind=kLoop, calls=%fused_computation.52 | loop fusion | bytes 7340032 | tf_op jit(solution)/shard_map/while/body/eval_jaxpr/slice | solution.py:65
  47.5 3.6 %copy.27 = bf16[4,896,256]{1,2,0:T(8,128)(2,1)} copy(bf16[4,896,256]{2,1,0:T(8,128)(2,1)} %get-tuple-element.18) | data formatting | bytes 3670016 | tf_op jit(solution)/shard_map/while/body/eval_jaxpr/slice | solution.py:66
  51.0 2.3 %copy.28 = bf16[4,896,256]{1,2,0:T(8,128)(2,1)} copy(bf16[4,896,256]{2,1,0:T(8,128)(2,1)S(1)} %get-tuple-element.17) | data formatting | bytes 3670016 | tf_op jit(solution)/shard_map/while/body/eval_jaxpr/slice | solution.py:65
  53.3 2.6 %bitcast_reduce_fusion = (f32[4,2,128]{2,1,0:T(2,128)S(1)}, f32[4,2,896,128]{3,2,1,0:T(8,128)S(1)}) fusion(pred[4,896]{1,0:T(4,128)(4,1)S(1)} %bitcast.82, bf16[4,896,2,128]{1,3,2,0:T(8,128)(2,1)} %bitcast.73, bf16[4,128,2,128]{1,3,2,0:T(8,128)(2,1)S(1)} %bitcast.80), kind=kOutput, calls=%fused_computation.2 | convolution fusion | flops 237632512 | bytes 5774848 | tf_op jit(solution)/shard_map/while/body/eval_jaxpr/qthd,qkhd->qhtk/dot_general | solution.py:68
  56.0 1.1 %fusion.1 = f32[4,2,128]{2,1,0:T(2,128)S(1)} fusion(f32[4,2,896,128]{3,2,1,0:T(8,128)S(1)} %get-tuple-element.32, f32[4,2,128]{2,1,0:T(2,128)S(1)} %get-tuple-element.30, pred[4,896]{1,0:T(4,128)(4,1)S(1)} %bitcast.83), kind=kLoop, calls=%fused_computation.5 | loop fusion | flops 3668992 | bytes 3681792 | tf_op jit(solution)/shard_map/while/body/eval_jaxpr/reduce_sum | solution.py:75
  57.1 1.3 %fusion.18 = bf16[4,128,2,128]{1,3,2,0:T(8,128)(2,1)S(1)} fusion(bf16[4,896,2,128]{1,3,2,0:T(8,128)(2,1)S(1)} %bitcast.77, f32[4,2,896,128]{3,2,1,0:T(8,128)S(1)} %get-tuple-element.32, f32[4,2,128]{2,1,0:T(2,128)S(1)} %get-tuple-element.30, pred[4,896]{1,0:T(4,128)(4,1)S(1)} %bitcast.84, f32[2,128]{1,0:T(2,128)S(1)} %broadcast_add_fusion, ...), kind=kOutput, calls=%fused_computation.16 | convolution fusion | flops 238944256 | bytes 5779968 | tf_op jit(solution)/shard_map/while/body/eval_jaxpr/qhtk,qkhd->qthd/dot_general | solution.py:77
  58.4 12.3 %all_to_all.54 = bf16[4,128,256]{1,2,0:T(8,128)(2,1)S(1)} all-to-all(bf16[4,128,256]{1,2,0:T(8,128)(2,1)S(1)} %bitcast.81), channel_id=1, replica_groups=mesh['groups'=2,'span'=4,'head'=4] {'head'}, dimensions={0} | all-to-all | bytes 524288 | tf_op jit(solution)/shard_map/all_to_all | solution.py:85
  70.7 0.8 %copy.39 = bf16[128,1024]{1,0:T(8,128)(2,1)} copy(bf16[128,1024]{0,1:T(8,128)(2,1)S(1)} %bitcast.78) | data formatting | bytes 524288 | tf_op jit(solution)/shard_map/all_to_all | solution.py:85
  (23 shorter events, 0.2 us)
Async XLA Ops:
  0.0 13.0 %copy-start = (bf16[256,256]{1,0:T(8,128)(2,1)S(1)}, bf16[256,256]{1,0:T(8,128)(2,1)}, u32[]{:S(2)}) copy-start(bf16[256,256]{1,0:T(8,128)(2,1)} %param.11) | copy-start | bytes 393220
  0.0 25.3 %copy-start.2 = (s32[4,7]{1,0:T(4,128)S(1)}, s32[4,7]{1,0:T(4,128)}, u32[]{:S(2)}) copy-start(s32[4,7]{1,0:T(4,128)} %param.9) | copy-start | bytes 340
  2.0 18.5 %all-to-all-start = ((bf16[128,4,256]{2,0,1:T(8,128)(2,1)}), bf16[128,4,256]{2,0,1:T(8,128)(2,1)S(1)}, u32[]{:S(2)}, u32[]{:S(2)}) async-start(bf16[128,4,256]{2,0,1:T(8,128)(2,1)} %copy.26), calls=%async_computation | async-start | bytes 524288 | tf_op jit(solution)/shard_map/all_to_all | solution.py:34
  7.7 7.4 %collective-permute-start = (bf16[128,256]{1,0:T(8,128)(2,1)S(1)}, bf16[128,256]{1,0:T(8,128)(2,1)S(1)}, u32[]{:S(2)}, u32[]{:S(2)}) collective-permute-start(bf16[128,256]{1,0:T(8,128)(2,1)S(1)} %get-tuple-element.28), channel_id=1, source_target_pairs={{0,3},{1,0},{2,1},{3,2},{4,7},{5,4},{6,5},{7,6},{8,11},{9,8},{10,9... | collective-permute-start | bytes 196616 | tf_op jit(solution)/shard_map/ppermute | solution.py:19
  11.0 9.4 %collective-permute-start.1 = (bf16[128,256]{1,0:T(8,128)(2,1)S(1)}, bf16[128,256]{1,0:T(8,128)(2,1)S(1)}, u32[]{:S(2)}, u32[]{:S(2)}) collective-permute-start(bf16[128,256]{1,0:T(8,128)(2,1)S(1)} %get-tuple-element.20), channel_id=1, source_target_pairs={{0,2},{1,3},{2,0},{3,1},{4,6},{5,7},{6,4},{7,5},{8,10},{9,11},{10,... | collective-permute-start | bytes 196616 | tf_op jit(solution)/shard_map/ppermute | solution.py:19
  11.0 9.4 %collective-permute-start.2 = (bf16[128,256]{1,0:T(8,128)(2,1)S(1)}, bf16[128,256]{1,0:T(8,128)(2,1)S(1)}, u32[]{:S(2)}, u32[]{:S(2)}) collective-permute-start(bf16[128,256]{1,0:T(8,128)(2,1)S(1)} %get-tuple-element.19), channel_id=1, source_target_pairs={{0,1},{1,2},{2,3},{3,0},{4,5},{5,6},{6,7},{7,4},{8,9},{9,10},{10,1... | collective-permute-start | bytes 196616 | tf_op jit(solution)/shard_map/ppermute | solution.py:19
  20.6 32.8 %all-to-all-start.1 = ((bf16[128,4,256]{0,2,1:T(8,128)(2,1)}), bf16[128,4,256]{0,2,1:T(8,128)(2,1)S(1)}, u32[]{:S(2)}, u32[]{:S(2)}) async-start(bf16[128,4,256]{0,2,1:T(8,128)(2,1)} %bitcast.7), calls=%async_computation.1 | async-start | bytes 524288 | tf_op jit(solution)/shard_map/all_to_all | solution.py:32
  24.0 17.1 %collective-permute-start.4 = (bf16[512,512]{1,0:T(8,128)(2,1)S(1)}, bf16[512,512]{1,0:T(8,128)(2,1)S(1)}, u32[]{:S(2)}, u32[]{:S(2)}) collective-permute-start(bf16[512,512]{1,0:T(8,128)(2,1)S(1)} %pad_maximum_fusion), channel_id=1, source_target_pairs={{0,4},{4,8},{8,12},{1,5},{5,9},{9,13},{2,6},{6,10},{10,14},{3,7},{... | collective-permute-start | bytes 1572872 | tf_op jit(solution)/shard_map/ppermute | solution.py:27
  25.5 15.7 %collective-permute-start.3 = (bf16[256,512]{1,0:T(8,128)(2,1)S(1)}, bf16[256,512]{1,0:T(8,128)(2,1)S(1)}, u32[]{:S(2)}, u32[]{:S(2)}) collective-permute-start(bf16[256,512]{1,0:T(8,128)(2,1)S(1)} %fusion.22), channel_id=1, source_target_pairs={{0,8},{4,12},{1,9},{5,13},{2,10},{6,14},{3,11},{7,15},{16,24},{20,... | collective-permute-start | bytes 786440 | tf_op jit(solution)/shard_map/ppermute | solution.py:27
  53.3 3.8 %copy-start.1 = (bf16[4,896,256]{1,2,0:T(8,128)(2,1)S(1)}, bf16[4,896,256]{1,2,0:T(8,128)(2,1)}, u32[]{:S(2)}) copy-start(bf16[4,896,256]{1,2,0:T(8,128)(2,1)} %copy.27) | copy-start | bytes 5505028
